TPU v7x, 256 devices: a whole 4x4x8 slice. The times are simulated.
256 devices in a mesh: seg: 4 (over x), pitch: 4 (over y), span: 16 (over z, core).
Axes of the slice: x: 4, y: 4, z: 8, core: 2. Of those that a mesh axis runs over, the one named last changes fastest.
Arguments:
- states: float32 [4, 5, 1024, 4096], P('seg', None, 'pitch', 'span'), may hold values from -6 to 6
- forcing: float32 [4, 5, 1024, 4096], P('seg', None, 'pitch', 'span'), may hold values from -6 to 6
- adv_pitch: float32 [5, 5], replicated, may hold values from -2.5 to 2.5
- adv_span: float32 [5, 5], replicated, may hold values from -2.5 to 2.5
- diffusion: float32 [5], replicated, may hold values from 0.1 to 0.4
Outputs:
- mismatch: float32 [4, 5, 1024, 4096], P('seg', None, 'pitch', 'span')
- gradient: float32 [4, 5, 1024, 4096], P('seg', None, 'pitch', 'span')
All inputs are finite; a program needn't handle non-finite values.
Results may differ from a plain program's by a relative error of at most 0.0001.
Values sent between devices are 32-bit elements; how exact they have to be, the bound alone decides.
A program may use at most 64 MiB of HBM per device.

v0:
```python
import functools

import jax
import jax.numpy as jnp
from jax import lax
from jax.experimental import pallas as pl
from jax.experimental.pallas import tpu as pltpu
from jax.sharding import PartitionSpec as P

MESH = pl.DeviceIdType.MESH
F = 5
L = 128
PAD = 16
CH = 32
M, E, H = 0, 1, 2


def along(axis, by):
    count = lax.axis_size(axis)
    return {axis: lax.rem(lax.axis_index(axis) + (by + count), count)}


def rolled(x, by):
    return pltpu.roll(x, by % L, 1)


def kernel(
    states, forcing, pitch_ref, span_ref, diff_ref, mis_out, grad_out,
    raw, force, v0, v1, w0, w1, end, got_a, got_b, packed, packed2, halo, halo2,
    load_s, load_f, a_send, a_recv, b_send, b_recv, col_send, col_recv, row_send, row_recv,
):
    rows = raw.shape[1]
    chunks = rows // CH
    blocks = rows // 8
    order = [0, chunks - 1] + list(range(1, chunks - 1))

    def load(src, dst, sem, c):
        part = pl.ds(c * CH, CH)
        return pltpu.make_async_copy(src.at[0, :, part], dst.at[:, part], sem.at[c])

    for c in range(chunks):
        load(states, raw, load_s, c).start()
    for c in range(chunks):
        load(forcing, force, load_f, c).start()

    barrier = pltpu.get_barrier_semaphore()
    for axis in ("seg", "pitch", "span"):
        for by in (1, -1):
            pl.semaphore_signal(barrier, inc=1, device_id=along(axis, by), device_id_type=MESH)

    lane = lax.broadcasted_iota(jnp.int32, (8, L), 1)
    low = lane < 64
    span_at, span_of = lax.axis_index("span"), lax.axis_size("span")
    has_left = jnp.where(span_at > 0, 1, 0)
    has_right = jnp.where(span_at < span_of - 1, 1, 0)
    inside = jnp.where(low, has_left, has_right) > 0
    packed_left = (lane & 3) >= 2
    packed_inside = jnp.where(packed_left, has_left, has_right) > 0

    fwd = (
        [[pitch_ref[f, g] * -0.125 for g in range(F)] for f in range(F)],
        [[span_ref[f, g] * -0.125 for g in range(F)] for f in range(F)],
    )
    adj = (
        [[pitch_ref[g, f] * 0.125 for g in range(F)] for f in range(F)],
        [[span_ref[g, f] * 0.125 for g in range(F)] for f in range(F)],
    )
    keep = [1.0 - diff_ref[f] for f in range(F)]
    visc = [diff_ref[f] * 0.25 for f in range(F)]

    def rotate_in(first, second):
        one, two = rolled(first, 64), rolled(second, 64)
        return jnp.where(low, one, two), jnp.where(low, two, one)

    def rotate_out(mid, edge):
        one, two = rolled(mid, 64), rolled(edge, 64)
        return jnp.where(low, two, one), jnp.where(low, one, two)

    def stencil(src, mats, e, outs, seam):
        along_pitch, along_span = mats
        total = {t: [None] * F for t in outs}
        for g in range(F):
            here, left, right = {}, {}, {}
            for t in (M, E, H):
                if (t == H and not seam) or (t == M and E not in outs and M not in outs):
                    continue
                here[t] = src[t, g, pl.ds(e, 8), :]
                right[t] = rolled(here[t], -1)
                left[t] = rolled(here[t], 1)
            for t in outs:
                if t == M:
                    rt = jnp.where(lane == 127, right[E], right[M])
                    lf = jnp.where(lane == 0, left[E], left[M])
                elif t == E:
                    rt = jnp.where(lane == 127, right[M], right[E])
                    lf = jnp.where(lane == 0, left[M], left[E])
                    if seam:
                        rt = jnp.where(lane == 63, right[H], rt)
                        lf = jnp.where(lane == 64, left[H], lf)
                else:
                    rt = jnp.where(lane == 63, right[E], right[H])
                    lf = jnp.where(lane == 64, left[E], left[H])
                up = src[t, g, pl.ds(e + 1, 8), :]
                dn = src[t, g, pl.ds(e - 1, 8), :]
                dp, ds = up - dn, rt - lf
                around = (up + dn) + (rt + lf)
                for f in range(F):
                    term = along_pitch[f][g] * dp + along_span[f][g] * ds
                    if f == g:
                        term = term + (keep[g] * here[t] + visc[g] * around)
                    total[t][f] = term if total[t][f] is None else total[t][f] + term
        return total

    def first_step(src, dst, mats, outs, seam, lo, hi):
        @pl.loop(lo, hi)
        def _(b):
            e = pl.multiple_of(b * 8 + PAD, 8)
            total = stencil(src, mats, e, outs, seam)
            for t in outs:
                for f in range(F):
                    value = total[t][f]
                    if t == H:
                        value = jnp.where(inside, value, 0.0)
                    dst[t, f, pl.ds(e, 8), :] = value

    def to_end(outs, lo, hi):
        @pl.loop(lo, hi)
        def _(b):
            e = pl.multiple_of(b * 8 + PAD, 8)
            r = pl.multiple_of(b * 8, 8)
            total = stencil(v1, fwd, e, outs, E in outs)
            for f in range(F):
                both = rotate_in(force[f, pl.ds(r, 8), 0:L], force[f, pl.ds(r, 8), L : 2 * L])
                for t in outs:
                    end[t, f, pl.ds(r, 8), :] = total[t][f] + 0.25 * both[t]

    def stream_a(t, c):
        return pltpu.make_async_remote_copy(
            src_ref=v0.at[t, :, pl.ds(pl.multiple_of(c * CH + PAD, 8), CH)],
            dst_ref=got_a.at[t, :, pl.ds(pl.multiple_of(c * CH, 8), CH)],
            send_sem=a_send.at[t, c], recv_sem=a_recv.at[t, c],
            device_id=along("seg", -1), device_id_type=MESH,
        )

    def stream_b(t, c):
        part = pl.ds(pl.multiple_of(c * CH, 8), CH)
        return pltpu.make_async_remote_copy(
            src_ref=end.at[t, :, part], dst_ref=got_b.at[t, :, part],
            send_sem=b_send.at[t, c], recv_sem=b_recv.at[t, c],
            device_id=along("seg", 1), device_id_type=MESH,
        )

    def columns(phase, side):
        source, target = ((packed, halo), (packed2, halo2))[phase]
        return pltpu.make_async_remote_copy(
            src_ref=source, dst_ref=target.at[side],
            send_sem=col_send.at[phase, side], recv_sem=col_recv.at[phase, side],
            device_id=along("span", (1, -1)[side]), device_id_type=MESH,
        )

    def edge_rows(phase, side):
        field = (v0, w0)[phase]
        if side == 0:
            src, dst = pl.ds(PAD + rows - 8, 8), pl.ds(PAD - 8, 8)
        else:
            src, dst = pl.ds(PAD, 8), pl.ds(PAD + rows, 8)
        return pltpu.make_async_remote_copy(
            src_ref=field.at[:, :, src], dst_ref=field.at[:, :, dst],
            send_sem=row_send.at[phase, side], recv_sem=row_recv.at[phase, side],
            device_id=along("pitch", (1, -1)[side]), device_id_type=MESH,
        )

    def pack(field, out):
        @pl.loop(0, blocks)
        def _(b):
            e = pl.multiple_of(b * 8 + PAD, 8)
            value = field[E, 2, pl.ds(e, 8), :]
            for f in (0, 1, 3, 4):
                at = 54 + 4 * f
                mine = (lane >= at) & (lane < at + 4)
                value = jnp.where(mine, rolled(field[E, f, pl.ds(e, 8), :], 4 * (f - 2)), value)
            out[pl.ds(pl.multiple_of(b * 8, 8), 8), :] = value

    def unpack(arrived, field):
        @pl.loop(0, blocks)
        def _(b):
            e = pl.multiple_of(b * 8 + PAD, 8)
            r = pl.multiple_of(b * 8, 8)
            value = jnp.where(packed_left, arrived[0, pl.ds(r, 8), :], arrived[1, pl.ds(r, 8), :])
            value = jnp.where(packed_inside, value, 0.0)
            for f in range(F):
                field[H, f, pl.ds(e, 8), :] = rolled(value, -4 * (f - 2))

    @pl.loop(0, chunks)
    def _(c):
        load(states, raw, load_s, c).wait()

        @pl.loop(0, CH // 8)
        def _(i):
            r = pl.multiple_of(c * CH + i * 8, 8)
            e = pl.multiple_of(r + PAD, 8)
            for f in range(F):
                mid, edge = rotate_in(raw[f, pl.ds(r, 8), 0:L], raw[f, pl.ds(r, 8), L : 2 * L])
                v0[M, f, pl.ds(e, 8), :] = mid
                v0[E, f, pl.ds(e, 8), :] = edge

    pack(v0, packed)
    pl.semaphore_wait(barrier, 6)
    for side in (0, 1):
        columns(0, side).start()
    for t in (E, M):
        for c in order:
            stream_a(t, c).start()
    for c in range(chunks):
        load(forcing, force, load_f, c).wait()

    per = CH // 8
    first_step(v0, v1, fwd, (M, E), False, per - 1, per + 1)

    @pl.loop(1, chunks - 1)
    def _(c):
        first_step(v0, v1, fwd, (M, E), False, c * per + 1, c * per + per + 1)
        to_end((M,), c * per, c * per + per)
        stream_b(M, c).start()

    for side in (0, 1):
        columns(0, side).wait()
    unpack(halo, v0)
    for side in (0, 1):
        edge_rows(0, side).start()
    first_step(v0, v1, fwd, (E, H), True, per - 1, blocks - per + 1)
    for side in (0, 1):
        edge_rows(0, side).wait()
    first_step(v0, v1, fwd, (M, E, H), True, -1, per - 1)
    first_step(v0, v1, fwd, (M, E, H), True, blocks - per + 1, blocks + 1)
    to_end((M, E), 0, per)
    stream_b(M, 0).start()
    stream_b(E, 0).start()

    @pl.loop(1, chunks - 1)
    def _(c):
        to_end((E,), c * per, c * per + per)
        stream_b(E, c).start()

    to_end((M, E), blocks - per, blocks)
    stream_b(M, chunks - 1).start()
    stream_b(E, chunks - 1).start()

    def arrive(t, c):
        stream_a(t, c).wait_recv()

        @pl.loop(c * per, c * per + per)
        def _(b):
            e = pl.multiple_of(b * 8 + PAD, 8)
            r = pl.multiple_of(b * 8, 8)
            for f in range(F):
                w0[t, f, pl.ds(e, 8), :] = end[t, f, pl.ds(r, 8), :] - got_a[t, f, pl.ds(r, 8), :]

    arrive(E, 0)
    arrive(E, chunks - 1)

    @pl.loop(1, chunks - 1)
    def _(c):
        arrive(E, c)

    pack(w0, packed2)
    for side in (0, 1):
        columns(1, side).start()
    arrive(M, 0)
    arrive(M, chunks - 1)
    for side in (0, 1):
        columns(1, side).wait()
    unpack(halo2, w0)
    for side in (0, 1):
        edge_rows(1, side).start()

    def out_rows(lo, hi):
        @pl.loop(lo, hi)
        def _(b):
            e = pl.multiple_of(b * 8 + PAD, 8)
            r = pl.multiple_of(b * 8, 8)
            for f in range(F):
                one, two = rotate_out(w0[M, f, pl.ds(e, 8), :], w0[E, f, pl.ds(e, 8), :])
                mis_out[0, f, pl.ds(r, 8), 0:L] = one
                mis_out[0, f, pl.ds(r, 8), L : 2 * L] = two

    def adjoint_rows(lo, hi):
        @pl.loop(lo, hi)
        def _(b):
            e = pl.multiple_of(b * 8 + PAD, 8)
            r = pl.multiple_of(b * 8, 8)
            total = stencil(w1, adj, e, (M, E), True)
            for f in range(F):
                parts = [
                    total[t][f] - (got_b[t, f, pl.ds(r, 8), :] - v0[t, f, pl.ds(e, 8), :])
                    for t in (M, E)
                ]
                one, two = rotate_out(*parts)
                grad_out[0, f, pl.ds(r, 8), 0:L] = one
                grad_out[0, f, pl.ds(r, 8), L : 2 * L] = two

    out_rows(0, per)
    out_rows(blocks - per, blocks)
    for side in (0, 1):
        edge_rows(1, side).wait()
    first_step(w0, w1, adj, (M, E, H), True, -1, per - 1)
    stream_b(M, 0).wait_recv()
    stream_b(E, 0).wait_recv()
    adjoint_rows(0, per - 2)

    @pl.loop(1, chunks - 1)
    def _(c):
        arrive(M, c)
        first_step(w0, w1, adj, (M, E, H), True, c * per - 1, c * per + per - 1)
        out_rows(c * per, c * per + per)
        stream_b(M, c).wait_recv()
        stream_b(E, c).wait_recv()
        adjoint_rows(c * per - 2, c * per + per - 2)

    first_step(w0, w1, adj, (M, E, H), True, blocks - per - 1, blocks + 1)
    stream_b(M, chunks - 1).wait_recv()
    stream_b(E, chunks - 1).wait_recv()
    adjoint_rows(blocks - per - 2, blocks)

    for t in (M, E):
        @pl.loop(0, chunks)
        def _(c):
            stream_a(t, c).wait_send()
            stream_b(t, c).wait_send()


def body(states, forcing, adv_pitch, adv_span, diffusion):
    rows = states.shape[2]
    chunks = rows // CH
    tall = rows + 2 * PAD
    shape = jax.ShapeDtypeStruct(states.shape, jnp.float32)
    dma = pltpu.SemaphoreType.DMA
    tiles = pltpu.VMEM((3, F, tall, L), jnp.float32)
    pair = pltpu.VMEM((2, F, rows, L), jnp.float32)
    block = pltpu.VMEM((F, rows, 2 * L), jnp.float32)
    return pl.pallas_call(
        kernel,
        out_shape=(shape, shape),
        in_specs=[pl.BlockSpec(memory_space=pltpu.HBM)] * 2 + [pl.BlockSpec(memory_space=pltpu.SMEM)] * 3,
        out_specs=[pl.BlockSpec(memory_space=pltpu.VMEM)] * 2,
        scratch_shapes=[
            block, block, tiles, tiles, tiles, tiles, pair, pair, pair,
            pltpu.VMEM((rows, L), jnp.float32), pltpu.VMEM((rows, L), jnp.float32),
            pltpu.VMEM((2, rows, L), jnp.float32), pltpu.VMEM((2, rows, L), jnp.float32),
            dma((chunks,)), dma((chunks,)),
            dma((2, chunks)), dma((2, chunks)), dma((2, chunks)), dma((2, chunks)),
            dma((2, 2)), dma((2, 2)), dma((2, 2)), dma((2, 2)),
        ],
        compiler_params=pltpu.CompilerParams(collective_id=0, has_side_effects=True, vmem_limit_bytes=40 << 20),
        name="orbit",
    )(states, forcing, adv_pitch, adv_span, diffusion)


def solution(mesh):
    spread = P("seg", None, "pitch", "span")
    return jax.shard_map(
        body,
        mesh=mesh,
        in_specs=(spread, spread, P(), P(), P()),
        out_specs=(spread, spread),
        check_vma=False,
    )
```

profile of v0, /device:TPU:97, one launch (start us, length us, event | category | flops | bytes accessed | tf_op | source)
XLA Modules:
  0.0 59.6 jit_solution(8758364416348007452)
XLA Ops:
  0.6 0.0 copy-start
  0.6 1.3 %copy-done = f32[1,5,256,256]{3,2,1,0:T(8,128)S(1)} copy-done((f32[1,5,256,256]{3,2,1,0:T(8,128)S(1)}, f32[1,5,256,256]{3,2,1,0:T(8,128)}, u32[]{:S(2)}) %copy-start) | copy-done | bytes 1310744
  1.9 0.0 copy-start.1
  2.0 1.3 %copy-done.1 = f32[1,5,256,256]{3,2,1,0:T(8,128)S(1)} copy-done((f32[1,5,256,256]{3,2,1,0:T(8,128)S(1)}, f32[1,5,256,256]{3,2,1,0:T(8,128)}, u32[]{:S(2)}) %copy-start.1) | copy-done | bytes 1310744
  3.3 0.0 copy-start.2
  3.3 0.7 %copy-done.2 = f32[5,5]{1,0:T(8,128)S(1)} copy-done((f32[5,5]{1,0:T(8,128)S(1)}, f32[5,5]{1,0:T(8,128)}, u32[]{:S(2)}) %copy-start.2) | copy-done | bytes 124
  4.0 0.0 copy-start.3
  4.0 0.7 %copy-done.3 = f32[5,5]{1,0:T(8,128)S(1)} copy-done((f32[5,5]{1,0:T(8,128)S(1)}, f32[5,5]{1,0:T(8,128)}, u32[]{:S(2)}) %copy-start.3) | copy-done | bytes 124
  4.6 0.0 copy-start.4
  4.6 0.7 %copy-done.4 = f32[5]{0:T(128)S(1)} copy-done((f32[5]{0:T(128)S(1)}, f32[5]{0:T(128)}, u32[]{:S(2)}) %copy-start.4) | copy-done | bytes 44
  5.3 52.2 %orbit.1 = (f32[1,5,256,256]{3,2,1,0:T(8,128)S(1)}, f32[1,5,256,256]{3,2,1,0:T(8,128)S(1)}) custom-call(f32[1,5,256,256]{3,2,1,0:T(8,128)S(1)} %copy-done, f32[1,5,256,256]{3,2,1,0:T(8,128)S(1)} %copy-done.1, f32[5,5]{1,0:T(8,128)S(1)} %copy-done.2, f32[5,5]{1,0:T(8,128)S(1)} %copy-done.3, f32[5]{0:T(128)S(1)} %copy-done.4), custom_call_target="tpu_custom_call" | custom-call | tf_op jit(solution)/shard_map/orbit/pallas_call | solution.py:341
  57.5 1.1 %copy.9 = f32[1,5,256,256]{3,2,1,0:T(8,128)} copy(f32[1,5,256,256]{3,2,1,0:T(8,128)S(1)} %get-tuple-element.4) | data formatting | bytes 2621440
  58.6 1.1 %copy.10 = f32[1,5,256,256]{3,2,1,0:T(8,128)} copy(f32[1,5,256,256]{3,2,1,0:T(8,128)S(1)} %get-tuple-element.5) | data formatting | bytes 2621440
Async XLA Ops:
  0.6 1.3 %copy-start = (f32[1,5,256,256]{3,2,1,0:T(8,128)S(1)}, f32[1,5,256,256]{3,2,1,0:T(8,128)}, u32[]{:S(2)}) copy-start(f32[1,5,256,256]{3,2,1,0:T(8,128)} %states.1) | copy-start | bytes 3932164
  1.9 1.3 %copy-start.1 = (f32[1,5,256,256]{3,2,1,0:T(8,128)S(1)}, f32[1,5,256,256]{3,2,1,0:T(8,128)}, u32[]{:S(2)}) copy-start(f32[1,5,256,256]{3,2,1,0:T(8,128)} %forcing.1) | copy-start | bytes 3932164
  3.3 0.7 %copy-start.2 = (f32[5,5]{1,0:T(8,128)S(1)}, f32[5,5]{1,0:T(8,128)}, u32[]{:S(2)}) copy-start(f32[5,5]{1,0:T(8,128)} %pitch_ref.1) | copy-start | bytes 304
  4.0 0.7 %copy-start.3 = (f32[5,5]{1,0:T(8,128)S(1)}, f32[5,5]{1,0:T(8,128)}, u32[]{:S(2)}) copy-start(f32[5,5]{1,0:T(8,128)} %span_ref.1) | copy-start | bytes 304
  4.6 0.7 %copy-start.4 = (f32[5]{0:T(128)S(1)}, f32[5]{0:T(128)}, u32[]{:S(2)}) copy-start(f32[5]{0:T(128)} %diff_ref.1) | copy-start | bytes 64
where the time goes:
time: 60.6 us; the launch traced here: 59.6 us
  Pallas kernels  52.2 us (86%)
  local copies, waits for them, and re-layouts  6.77 us (11%)
  between operations  0.65 us (1%)
    pallas_call x1, Pallas kernels, body(): pl.pallas_call(kernel, out_shape=(shape, shape), in_specs=[pl.BlockSpec(m...  52.2 us
    unnamed x12, local copies, waits for them, and re-layouts  6.77 us

commit v1 on v0

v1 whole, which is shorter than its diff:
```python
import functools

import jax
import jax.numpy as jnp
from jax import lax
from jax.experimental import pallas as pl
from jax.experimental.pallas import tpu as pltpu
from jax.sharding import PartitionSpec as P

MESH = pl.DeviceIdType.MESH
F = 5
L = 128
PAD = 16
CH = 32
M, E, H = 0, 1, 2


def along(axis, by):
    count = lax.axis_size(axis)
    return {axis: lax.rem(lax.axis_index(axis) + (by + count), count)}


def rolled(x, by):
    return pltpu.roll(x, by % L, 1)


def kernel(
    states, forcing, pitch_ref, span_ref, diff_ref, mis_out, grad_out,
    raw, force, across, v0, v1, w0, w1, end, got_a, got_b, packed, packed2, halo, halo2,
    load_s, load_f, a_send, a_recv, b_send, b_recv, col_send, col_recv, row_send, row_recv,
):
    rows = raw.shape[1]
    chunks = rows // CH
    blocks = rows // 8
    order = [0, chunks - 1] + list(range(1, chunks - 1))

    def load(src, dst, sem, c):
        part = pl.ds(c * CH, CH)
        return pltpu.make_async_copy(src.at[0, :, part], dst.at[:, part], sem.at[c])

    for c in range(chunks):
        load(states, raw, load_s, c).start()
    for c in range(chunks):
        load(forcing, force, load_f, c).start()

    barrier = pltpu.get_barrier_semaphore()
    for axis in ("seg", "pitch", "span"):
        for by in (1, -1):
            pl.semaphore_signal(barrier, inc=1, device_id=along(axis, by), device_id_type=MESH)

    lane = lax.broadcasted_iota(jnp.int32, (8, L), 1)
    low = lane < 64
    span_at, span_of = lax.axis_index("span"), lax.axis_size("span")
    has_left = jnp.where(span_at > 0, 1, 0)
    has_right = jnp.where(span_at < span_of - 1, 1, 0)
    inside = jnp.where(low, has_left, has_right) > 0
    packed_left = (lane & 3) >= 2
    packed_inside = jnp.where(packed_left, has_left, has_right) > 0

    fwd = (
        [[pitch_ref[f, g] * -0.125 for g in range(F)] for f in range(F)],
        [[span_ref[f, g] * -0.125 for g in range(F)] for f in range(F)],
    )
    adj = (
        [[pitch_ref[g, f] * 0.125 for g in range(F)] for f in range(F)],
        [[span_ref[g, f] * 0.125 for g in range(F)] for f in range(F)],
    )
    keep = [1.0 - diff_ref[f] for f in range(F)]
    visc = [diff_ref[f] * 0.25 for f in range(F)]

    def rotate_in(first, second):
        one, two = rolled(first, 64), rolled(second, 64)
        return jnp.where(low, one, two), jnp.where(low, two, one)

    def rotate_out(mid, edge):
        one, two = rolled(mid, 64), rolled(edge, 64)
        return jnp.where(low, two, one), jnp.where(low, one, two)

    def steps(lo, count, run, size=4):
        if count // size:
            @pl.loop(0, count // size)
            def _(i):
                run(lo + i * size, size)
        if count % size:
            run(lo + count // size * size, count % size)

    def row_at(b, pad=PAD):
        return pl.multiple_of(b * 8 + pad, 8)

    def stencil(src, mats, b, n, outs, seam, emit):
        along_pitch, along_span = mats
        for u in range(n):
            part = slice(u * 8, u * 8 + 8)
            for g in range(F):
                right, left = {}, {}
                for t in (M, E, H) if seam else (M, E):
                    here = src[t, g, pl.ds(row_at(b + u), 8), :]
                    right[t] = rolled(here, -1)
                    left[t] = rolled(here, 1)
                for t in outs:
                    if t == M:
                        rt = jnp.where(lane == 127, right[E], right[M])
                        lf = jnp.where(lane == 0, left[E], left[M])
                    elif t == E:
                        rt = jnp.where(lane == 127, right[M], right[E])
                        lf = jnp.where(lane == 0, left[M], left[E])
                        if seam:
                            rt = jnp.where(lane == 63, right[H], rt)
                            lf = jnp.where(lane == 64, left[H], lf)
                    else:
                        rt = jnp.where(lane == 63, right[E], right[H])
                        lf = jnp.where(lane == 64, left[E], left[H])
                    across[0, t, g, part, :] = rt - lf
                    across[1, t, g, part, :] = rt + lf
        for u in range(n):
            e = row_at(b + u)
            part = slice(u * 8, u * 8 + 8)
            total = {t: [None] * F for t in outs}
            for g in range(F):
                for t in outs:
                    up = src[t, g, pl.ds(e + 1, 8), :]
                    dn = src[t, g, pl.ds(e - 1, 8), :]
                    dp, ds = up - dn, across[0, t, g, part, :]
                    around = (up + dn) + across[1, t, g, part, :]
                    for f in range(F):
                        term = along_pitch[f][g] * dp + along_span[f][g] * ds
                        if f == g:
                            term = term + (keep[g] * src[t, g, pl.ds(e, 8), :] + visc[g] * around)
                        total[t][f] = term if total[t][f] is None else total[t][f] + term
            emit(b + u, total)

    def first_step(src, dst, mats, outs, seam, lo, count):
        def emit(b, total):
            for t in outs:
                for f in range(F):
                    value = total[t][f]
                    if t == H:
                        value = jnp.where(inside, value, 0.0)
                    dst[t, f, pl.ds(row_at(b), 8), :] = value

        steps(lo, count, lambda b, n: stencil(src, mats, b, n, outs, seam, emit))

    def to_end(outs, fresh, lo, count):
        def emit(b, total):
            part = pl.ds(row_at(b, 0), 8)
            for f in range(F):
                for t in outs:
                    end[t, f, part, :] = total[t][f] + end[t, f, part, :]

        def run(b, n):
            if fresh:
                for u in range(n):
                    part = pl.ds(row_at(b + u, 0), 8)
                    for f in range(F):
                        both = rotate_in(force[f, part, 0:L], force[f, part, L : 2 * L])
                        end[M, f, part, :] = 0.25 * both[M]
                        end[E, f, part, :] = 0.25 * both[E]
            stencil(v1, fwd, b, n, outs, E in outs, emit)

        steps(lo, count, run)

    def stream_a(t, c):
        return pltpu.make_async_remote_copy(
            src_ref=v0.at[t, :, pl.ds(pl.multiple_of(c * CH + PAD, 8), CH)],
            dst_ref=got_a.at[t, :, pl.ds(pl.multiple_of(c * CH, 8), CH)],
            send_sem=a_send.at[t, c], recv_sem=a_recv.at[t, c],
            device_id=along("seg", -1), device_id_type=MESH,
        )

    def stream_b(t, c):
        part = pl.ds(pl.multiple_of(c * CH, 8), CH)
        return pltpu.make_async_remote_copy(
            src_ref=end.at[t, :, part], dst_ref=got_b.at[t, :, part],
            send_sem=b_send.at[t, c], recv_sem=b_recv.at[t, c],
            device_id=along("seg", 1), device_id_type=MESH,
        )

    def columns(phase, side):
        source, target = ((packed, halo), (packed2, halo2))[phase]
        return pltpu.make_async_remote_copy(
            src_ref=source, dst_ref=target.at[side],
            send_sem=col_send.at[phase, side], recv_sem=col_recv.at[phase, side],
            device_id=along("span", (1, -1)[side]), device_id_type=MESH,
        )

    def edge_rows(phase, side):
        field = (v0, w0)[phase]
        if side == 0:
            src, dst = pl.ds(PAD + rows - 8, 8), pl.ds(PAD - 8, 8)
        else:
            src, dst = pl.ds(PAD, 8), pl.ds(PAD + rows, 8)
        return pltpu.make_async_remote_copy(
            src_ref=field.at[:, :, src], dst_ref=field.at[:, :, dst],
            send_sem=row_send.at[phase, side], recv_sem=row_recv.at[phase, side],
            device_id=along("pitch", (1, -1)[side]), device_id_type=MESH,
        )

    def pack(field, out):
        def run(b, n):
            for u in range(n):
                value = field[E, 2, pl.ds(row_at(b + u), 8), :]
                for f in (0, 1, 3, 4):
                    at = 54 + 4 * f
                    mine = (lane >= at) & (lane < at + 4)
                    value = jnp.where(mine, rolled(field[E, f, pl.ds(row_at(b + u), 8), :], 4 * (f - 2)), value)
                out[pl.ds(row_at(b + u, 0), 8), :] = value

        steps(0, blocks, run, 8)

    def unpack(arrived, field):
        def run(b, n):
            for u in range(n):
                part = pl.ds(row_at(b + u, 0), 8)
                value = jnp.where(packed_left, arrived[0, part, :], arrived[1, part, :])
                value = jnp.where(packed_inside, value, 0.0)
                for f in range(F):
                    field[H, f, pl.ds(row_at(b + u), 8), :] = rolled(value, -4 * (f - 2))

        steps(0, blocks, run, 8)

    per = CH // 8

    @pl.loop(0, chunks)
    def _(c):
        load(states, raw, load_s, c).wait()
        for u in range(per):
            b = c * per + u
            part = pl.ds(row_at(b, 0), 8)
            for f in range(F):
                mid, edge = rotate_in(raw[f, part, 0:L], raw[f, part, L : 2 * L])
                v0[M, f, pl.ds(row_at(b), 8), :] = mid
                v0[E, f, pl.ds(row_at(b), 8), :] = edge

    pack(v0, packed)
    pl.semaphore_wait(barrier, 6)
    for side in (0, 1):
        columns(0, side).start()
    for t in (E, M):
        for c in order:
            stream_a(t, c).start()
    for c in range(chunks):
        load(forcing, force, load_f, c).wait()

    first_step(v0, v1, fwd, (M, E), False, per - 1, 2)

    @pl.loop(1, chunks - 1)
    def _(c):
        first_step(v0, v1, fwd, (M, E), False, c * per + 1, per)
        to_end((M,), True, c * per, per)
        stream_b(M, c).start()

    for side in (0, 1):
        columns(0, side).wait()
    unpack(halo, v0)
    for side in (0, 1):
        edge_rows(0, side).start()
    first_step(v0, v1, fwd, (E, H), True, per - 1, blocks - 2 * per + 2)
    for side in (0, 1):
        edge_rows(0, side).wait()

    @pl.loop(0, 2)
    def _(i):
        first_step(v0, v1, fwd, (M, E, H), True, i * (blocks - per + 2) - 1, per)

    def both_ends(c):
        to_end((M, E), True, c * per, per)
        stream_b(M, c).start()
        stream_b(E, c).start()

    both_ends(0)

    @pl.loop(1, chunks - 1)
    def _(c):
        to_end((E,), False, c * per, per)
        stream_b(E, c).start()

    both_ends(chunks - 1)

    def arrive(t, c):
        stream_a(t, c).wait_recv()

        for u in range(per):
            b = c * per + u
            part = pl.ds(row_at(b, 0), 8)
            for f in range(F):
                w0[t, f, pl.ds(row_at(b), 8), :] = end[t, f, part, :] - got_a[t, f, part, :]

    arrive(E, 0)
    arrive(E, chunks - 1)

    @pl.loop(1, chunks - 1)
    def _(c):
        arrive(E, c)

    pack(w0, packed2)
    for side in (0, 1):
        columns(1, side).start()
    arrive(M, 0)
    arrive(M, chunks - 1)
    for side in (0, 1):
        columns(1, side).wait()
    unpack(halo2, w0)
    for side in (0, 1):
        edge_rows(1, side).start()

    def out_rows(lo, count):
        def run(b, n):
            for u in range(n):
                part = pl.ds(row_at(b + u, 0), 8)
                for f in range(F):
                    one, two = rotate_out(*[w0[t, f, pl.ds(row_at(b + u), 8), :] for t in (M, E)])
                    mis_out[0, f, part, 0:L] = one
                    mis_out[0, f, part, L : 2 * L] = two

        steps(lo, count, run)

    def adjoint_rows(lo, count):
        def emit(b, total):
            part = pl.ds(row_at(b, 0), 8)
            for f in range(F):
                one, two = rotate_out(*[
                    total[t][f] - (got_b[t, f, part, :] - v0[t, f, pl.ds(row_at(b), 8), :]) for t in (M, E)
                ])
                grad_out[0, f, part, 0:L] = one
                grad_out[0, f, part, L : 2 * L] = two

        steps(lo, count, lambda b, n: stencil(w1, adj, b, n, (M, E), True, emit))

    for side in (0, 1):
        edge_rows(1, side).wait()
    first_step(w0, w1, adj, (M, E, H), True, -1, per)
    out_rows(0, per)
    stream_b(M, 0).wait_recv()
    stream_b(E, 0).wait_recv()
    adjoint_rows(0, per - 2)

    @pl.loop(1, chunks - 1)
    def _(c):
        arrive(M, c)
        first_step(w0, w1, adj, (M, E, H), True, c * per - 1, per)
        out_rows(c * per, per)
        stream_b(M, c).wait_recv()
        stream_b(E, c).wait_recv()
        adjoint_rows(c * per - 2, per)

    first_step(w0, w1, adj, (M, E, H), True, blocks - per - 1, per + 2)
    out_rows(blocks - per, per)
    stream_b(M, chunks - 1).wait_recv()
    stream_b(E, chunks - 1).wait_recv()
    adjoint_rows(blocks - per - 2, per + 2)

    for t in (M, E):
        @pl.loop(0, chunks)
        def _(c):
            stream_a(t, c).wait_send()
            stream_b(t, c).wait_send()


def body(states, forcing, adv_pitch, adv_span, diffusion):
    states, forcing, adv_pitch, adv_span, diffusion = (
        pltpu.with_memory_space_constraint(x, pltpu.HBM) for x in (states, forcing, adv_pitch, adv_span, diffusion)
    )
    rows = states.shape[2]
    chunks = rows // CH
    tall = rows + 2 * PAD
    shape = jax.ShapeDtypeStruct(states.shape, jnp.float32)
    dma = pltpu.SemaphoreType.DMA
    tiles = pltpu.VMEM((3, F, tall, L), jnp.float32)
    pair = pltpu.VMEM((2, F, rows, L), jnp.float32)
    block = pltpu.VMEM((F, rows, 2 * L), jnp.float32)
    return pl.pallas_call(
        kernel,
        out_shape=(shape, shape),
        in_specs=[pl.BlockSpec(memory_space=pltpu.HBM)] * 2 + [pl.BlockSpec(memory_space=pltpu.SMEM)] * 3,
        out_specs=[pl.BlockSpec(memory_space=pltpu.VMEM)] * 2,
        scratch_shapes=[
            block, block, pltpu.VMEM((2, 3, F, CH, L), jnp.float32), tiles, tiles, tiles, tiles, pair, pair, pair,
            pltpu.VMEM((rows, L), jnp.float32), pltpu.VMEM((rows, L), jnp.float32),
            pltpu.VMEM((2, rows, L), jnp.float32), pltpu.VMEM((2, rows, L), jnp.float32),
            dma((chunks,)), dma((chunks,)),
            dma((2, chunks)), dma((2, chunks)), dma((2, chunks)), dma((2, chunks)),
            dma((2, 2)), dma((2, 2)), dma((2, 2)), dma((2, 2)),
        ],
        compiler_params=pltpu.CompilerParams(collective_id=0, has_side_effects=True, vmem_limit_bytes=40 << 20),
        name="orbit",
    )(states, forcing, adv_pitch, adv_span, diffusion)


def solution(mesh):
    spread = P("seg", None, "pitch", "span")
    return jax.shard_map(
        body,
        mesh=mesh,
        in_specs=(spread, spread, P(), P(), P()),
        out_specs=(spread, spread),
        check_vma=False,
    )
```

time: 60.6 us -> 42.4 us (0.70)
  the two profiles are of different devices: /device:TPU:97 before, /device:TPU:2 now
where the time goes in v1:
time: 42.4 us; the launch traced here: 42.2 us
  Pallas kernels  39.5 us (93%)
  local copies, waits for them, and re-layouts  2.11 us (5%)
  between operations  0.64 us (2%)
    pallas_call x1, Pallas kernels, body(): pl.pallas_call(kernel, out_shape=(shape, shape), in_specs=[pl.BlockSpec(m...  39.5 us
    unnamed x2, local copies, waits for them, and re-layouts  2.11 us

profile of v1, /device:TPU:2, one launch (start us, length us, event | category | flops | bytes accessed | tf_op | source)
XLA Modules:
  0.0 42.2 jit_solution(10292223307781771341)
XLA Ops:
  0.6 39.5 %orbit.1 = (f32[1,5,256,256]{3,2,1,0:T(8,128)S(1)}, f32[1,5,256,256]{3,2,1,0:T(8,128)S(1)}) custom-call(f32[1,5,256,256]{3,2,1,0:T(8,128)} %states.1, f32[1,5,256,256]{3,2,1,0:T(8,128)} %forcing.1, f32[5,5]{1,0:T(8,128)} %pitch_ref.1, f32[5,5]{1,0:T(8,128)} %span_ref.1, f32[5]{0:T(128)} %diff_ref.1), custom_call_target="tpu_custom_call" | custom-call | tf_op jit(solution)/shard_map/orbit/pallas_call | solution.py:371
  40.1 1.1 %copy.9 = f32[1,5,256,256]{3,2,1,0:T(8,128)} copy(f32[1,5,256,256]{3,2,1,0:T(8,128)S(1)} %get-tuple-element.4) | data formatting | bytes 2621440
  41.2 1.1 %copy.10 = f32[1,5,256,256]{3,2,1,0:T(8,128)} copy(f32[1,5,256,256]{3,2,1,0:T(8,128)S(1)} %get-tuple-element.5) | data formatting | bytes 2621440

commit v2 on v1

--- a/solution.py
+++ b/solution.py
@@ -25,14 +25,16 @@
 
 
 def kernel(
-    states, forcing, pitch_ref, span_ref, diff_ref, mis_out, grad_out,
-    raw, force, across, v0, v1, w0, w1, end, got_a, got_b, packed, packed2, halo, halo2,
-    load_s, load_f, a_send, a_recv, b_send, b_recv, col_send, col_recv, row_send, row_recv,
+    states, forcing, pitch_hbm, span_hbm, diff_hbm, mis_out, grad_out,
+    pitch_ref, span_ref, diff_ref, raw, force, across, v0, v1, w0, w1, end, got_a, got_b, packed, packed2, halo, halo2,
+    load_c, load_s, load_f, a_send, a_recv, b_send, b_recv, col_send, col_recv, row_send, row_recv,
 ):
     rows = raw.shape[1]
     chunks = rows // CH
     blocks = rows // 8
-    order = [0, chunks - 1] + list(range(1, chunks - 1))
+    per = CH // 8
+    half = chunks // 2
+    outer_first = [c for i in range(half) for c in (i, chunks - 1 - i)]
 
     def load(src, dst, sem, c):
         part = pl.ds(c * CH, CH)
@@ -40,8 +42,12 @@
 
     for c in range(chunks):
         load(states, raw, load_s, c).start()
-    for c in range(chunks):
-        load(forcing, force, load_f, c).start()
+    coefs = [
+        pltpu.make_async_copy(src, dst, load_c.at[i])
+        for i, (src, dst) in enumerate(((pitch_hbm, pitch_ref), (span_hbm, span_ref), (diff_hbm, diff_ref)))
+    ]
+    for copy in coefs:
+        copy.start()
 
     barrier = pltpu.get_barrier_semaphore()
     for axis in ("seg", "pitch", "span"):
@@ -56,17 +62,6 @@
     inside = jnp.where(low, has_left, has_right) > 0
     packed_left = (lane & 3) >= 2
     packed_inside = jnp.where(packed_left, has_left, has_right) > 0
-
-    fwd = (
-        [[pitch_ref[f, g] * -0.125 for g in range(F)] for f in range(F)],
-        [[span_ref[f, g] * -0.125 for g in range(F)] for f in range(F)],
-    )
-    adj = (
-        [[pitch_ref[g, f] * 0.125 for g in range(F)] for f in range(F)],
-        [[span_ref[g, f] * 0.125 for g in range(F)] for f in range(F)],
-    )
-    keep = [1.0 - diff_ref[f] for f in range(F)]
-    visc = [diff_ref[f] * 0.25 for f in range(F)]
 
     def rotate_in(first, second):
         one, two = rolled(first, 64), rolled(second, 64)
@@ -218,8 +213,6 @@
 
         steps(0, blocks, run, 8)
 
-    per = CH // 8
-
     @pl.loop(0, chunks)
     def _(c):
         load(states, raw, load_s, c).wait()
@@ -231,15 +224,31 @@
                 v0[M, f, pl.ds(row_at(b), 8), :] = mid
                 v0[E, f, pl.ds(row_at(b), 8), :] = edge
 
+    for c in range(chunks):
+        load(forcing, force, load_f, c).start()
+    pl.semaphore_wait(barrier, 6)
+    for c in outer_first:
+        stream_a(E, c).start()
     pack(v0, packed)
-    pl.semaphore_wait(barrier, 6)
     for side in (0, 1):
         columns(0, side).start()
-    for t in (E, M):
-        for c in order:
-            stream_a(t, c).start()
+    for c in outer_first:
+        stream_a(M, c).start()
+    for copy in coefs:
+        copy.wait()
     for c in range(chunks):
         load(forcing, force, load_f, c).wait()
+
+    fwd = (
+        [[pitch_ref[f, g] * -0.125 for g in range(F)] for f in range(F)],
+        [[span_ref[f, g] * -0.125 for g in range(F)] for f in range(F)],
+    )
+    adj = (
+        [[pitch_ref[g, f] * 0.125 for g in range(F)] for f in range(F)],
+        [[span_ref[g, f] * 0.125 for g in range(F)] for f in range(F)],
+    )
+    keep = [1.0 - diff_ref[f] for f in range(F)]
+    visc = [diff_ref[f] * 0.25 for f in range(F)]
 
     first_step(v0, v1, fwd, (M, E), False, per - 1, 2)
 
@@ -268,13 +277,17 @@
         stream_b(E, c).start()
 
     both_ends(0)
-
-    @pl.loop(1, chunks - 1)
-    def _(c):
+    both_ends(chunks - 1)
+
+    def inward(j):
+        lower = j % 2
+        return 1 + j // 2 + lower * (chunks - 3 - j // 2 * 2), lower
+
+    @pl.loop(0, chunks - 2)
+    def _(j):
+        c, _ = inward(j)
         to_end((E,), False, c * per, per)
         stream_b(E, c).start()
-
-    both_ends(chunks - 1)
 
     def arrive(t, c):
         stream_a(t, c).wait_recv()
@@ -328,26 +341,50 @@
 
     for side in (0, 1):
         edge_rows(1, side).wait()
-    first_step(w0, w1, adj, (M, E, H), True, -1, per)
-    out_rows(0, per)
-    stream_b(M, 0).wait_recv()
-    stream_b(E, 0).wait_recv()
-    adjoint_rows(0, per - 2)
-
-    @pl.loop(1, chunks - 1)
-    def _(c):
-        arrive(M, c)
-        first_step(w0, w1, adj, (M, E, H), True, c * per - 1, per)
-        out_rows(c * per, per)
+    def arrive_b(c):
         stream_b(M, c).wait_recv()
         stream_b(E, c).wait_recv()
-        adjoint_rows(c * per - 2, per)
-
-    first_step(w0, w1, adj, (M, E, H), True, blocks - per - 1, per + 2)
-    out_rows(blocks - per, per)
-    stream_b(M, chunks - 1).wait_recv()
-    stream_b(E, chunks - 1).wait_recv()
-    adjoint_rows(blocks - per - 2, per + 2)
+
+    @pl.loop(0, 2)
+    def _(i):
+        first_step(w0, w1, adj, (M, E, H), True, i * (blocks - per + 2) - 1, per)
+        out_rows(i * (blocks - per), per)
+        arrive_b(i * (chunks - 1))
+        adjoint_rows(i * (blocks - per + 2), per - 2)
+
+    @pl.loop(0, chunks - 3)
+    def _(j):
+        c, lower = inward(j)
+        arrive(M, c)
+        first_step(w0, w1, adj, (M, E, H), True, c * per - 1 + 2 * lower, per)
+        out_rows(c * per, per)
+        arrive_b(c)
+        adjoint_rows(c * per - 2 + 4 * lower, per)
+
+    arrive(M, half)
+    first_step(w0, w1, adj, (M, E, H), True, half * per - 1, per + 2)
+    out_rows(half * per, per)
+
+    def keep_adjoint(b, total):
+        for f in range(F):
+            for t in (M, E):
+                w0[t, f, pl.ds(row_at(b), 8), :] = total[t][f]
+
+    steps(half * per - 2, per + 4, lambda b, n: stencil(w1, adj, b, n, (M, E), True, keep_adjoint))
+    arrive_b(half)
+
+    def last_rows(b, n):
+        for u in range(n):
+            part = pl.ds(row_at(b + u, 0), 8)
+            tall = pl.ds(row_at(b + u), 8)
+            for f in range(F):
+                one, two = rotate_out(*[
+                    w0[t, f, tall, :] - (got_b[t, f, part, :] - v0[t, f, tall, :]) for t in (M, E)
+                ])
+                grad_out[0, f, part, 0:L] = one
+                grad_out[0, f, part, L : 2 * L] = two
+
+    steps(half * per - 2, per + 4, last_rows)
 
     for t in (M, E):
         @pl.loop(0, chunks)
@@ -371,13 +408,14 @@
     return pl.pallas_call(
         kernel,
         out_shape=(shape, shape),
-        in_specs=[pl.BlockSpec(memory_space=pltpu.HBM)] * 2 + [pl.BlockSpec(memory_space=pltpu.SMEM)] * 3,
+        in_specs=[pl.BlockSpec(memory_space=pltpu.HBM)] * 5,
         out_specs=[pl.BlockSpec(memory_space=pltpu.VMEM)] * 2,
         scratch_shapes=[
+            pltpu.SMEM((F, F), jnp.float32), pltpu.SMEM((F, F), jnp.float32), pltpu.SMEM((F,), jnp.float32),
             block, block, pltpu.VMEM((2, 3, F, CH, L), jnp.float32), tiles, tiles, tiles, tiles, pair, pair, pair,
             pltpu.VMEM((rows, L), jnp.float32), pltpu.VMEM((rows, L), jnp.float32),
             pltpu.VMEM((2, rows, L), jnp.float32), pltpu.VMEM((2, rows, L), jnp.float32),
-            dma((chunks,)), dma((chunks,)),
+            dma((3,)), dma((chunks,)), dma((chunks,)),
             dma((2, chunks)), dma((2, chunks)), dma((2, chunks)), dma((2, chunks)),
             dma((2, 2)), dma((2, 2)), dma((2, 2)), dma((2, 2)),
         ],

time: 42.4 us -> 41.7 us (0.983)
  Pallas kernels: 39.5 us -> 38.8 us
    pallas_call x1, Pallas kernels: 39.5 us -> 38.8 us  [body(): pl.pallas_call(kernel, out_shape=(shape, shape), in_specs=[pl.BlockSpec(m...]
where the time goes in v2:
time: 41.7 us; the launch traced here: 41.6 us
  Pallas kernels  38.8 us (93%)
  local copies, waits for them, and re-layouts  2.11 us (5%)
  between operations  0.64 us (2%)
    pallas_call x1, Pallas kernels, body(): pl.pallas_call(kernel, out_shape=(shape, shape), in_specs=[pl.BlockSpec(m...  38.8 us
    unnamed x2, local copies, waits for them, and re-layouts  2.11 us

profile of v2, /device:TPU:2, one launch (start us, length us, event | category | flops | bytes accessed | tf_op | source)
XLA Modules:
  0.0 41.6 jit_solution(12267255535248619395)
XLA Ops:
  0.6 38.8 %orbit.1 = (f32[1,5,256,256]{3,2,1,0:T(8,128)S(1)}, f32[1,5,256,256]{3,2,1,0:T(8,128)S(1)}) custom-call(f32[1,5,256,256]{3,2,1,0:T(8,128)} %states.1, f32[1,5,256,256]{3,2,1,0:T(8,128)} %forcing.1, f32[5,5]{1,0:T(8,128)} %pitch_hbm.1, f32[5,5]{1,0:T(8,128)} %span_hbm.1, f32[5]{0:T(128)} %diff_hbm.1), custom_call_target="tpu_custom_call" | custom-call | tf_op jit(solution)/shard_map/orbit/pallas_call | solution.py:408
  39.5 1.1 %copy.9 = f32[1,5,256,256]{3,2,1,0:T(8,128)} copy(f32[1,5,256,256]{3,2,1,0:T(8,128)S(1)} %get-tuple-element.4) | data formatting | bytes 2621440
  40.5 1.1 %copy.10 = f32[1,5,256,256]{3,2,1,0:T(8,128)} copy(f32[1,5,256,256]{3,2,1,0:T(8,128)S(1)} %get-tuple-element.5) | data formatting | bytes 2621440

commit v3 on v2

--- a/solution.py
+++ b/solution.py
@@ -27,14 +27,16 @@
 def kernel(
     states, forcing, pitch_hbm, span_hbm, diff_hbm, mis_out, grad_out,
     pitch_ref, span_ref, diff_ref, raw, force, across, v0, v1, w0, w1, end, got_a, got_b, packed, packed2, halo, halo2,
-    load_c, load_s, load_f, a_send, a_recv, b_send, b_recv, col_send, col_recv, row_send, row_recv,
+    load_c, load_s, load_f, a_send, a_recv, b_send, b_recv, col_send, col_recv, pair_send, pair_recv, row_send, row_recv,
 ):
     rows = raw.shape[1]
     chunks = rows // CH
+    assert chunks == 8
     blocks = rows // 8
     per = CH // 8
     half = chunks // 2
     outer_first = [c for i in range(half) for c in (i, chunks - 1 - i)]
+    a_order = [(t, c) for part in (outer_first[:2], outer_first[2:]) for t in (E, M) for c in part]
 
     def load(src, dst, sem, c):
         part = pl.ds(c * CH, CH)
@@ -170,11 +172,17 @@
             device_id=along("seg", 1), device_id_type=MESH,
         )
 
-    def columns(phase, side):
-        source, target = ((packed, halo), (packed2, halo2))[phase]
+    def columns(side):
         return pltpu.make_async_remote_copy(
-            src_ref=source, dst_ref=target.at[side],
-            send_sem=col_send.at[phase, side], recv_sem=col_recv.at[phase, side],
+            src_ref=packed, dst_ref=halo.at[side],
+            send_sem=col_send.at[side], recv_sem=col_recv.at[side],
+            device_id=along("span", (1, -1)[side]), device_id_type=MESH,
+        )
+
+    def pair_columns(k, side):
+        return pltpu.make_async_remote_copy(
+            src_ref=packed2.at[k], dst_ref=halo2.at[side, k],
+            send_sem=pair_send.at[k, side], recv_sem=pair_recv.at[k, side],
             device_id=along("span", (1, -1)[side]), device_id_type=MESH,
         )
 
@@ -190,28 +198,46 @@
             device_id=along("pitch", (1, -1)[side]), device_id_type=MESH,
         )
 
-    def pack(field, out):
-        def run(b, n):
-            for u in range(n):
-                value = field[E, 2, pl.ds(row_at(b + u), 8), :]
-                for f in (0, 1, 3, 4):
-                    at = 54 + 4 * f
-                    mine = (lane >= at) & (lane < at + 4)
-                    value = jnp.where(mine, rolled(field[E, f, pl.ds(row_at(b + u), 8), :], 4 * (f - 2)), value)
-                out[pl.ds(row_at(b + u, 0), 8), :] = value
-
-        steps(0, blocks, run, 8)
-
-    def unpack(arrived, field):
-        def run(b, n):
-            for u in range(n):
-                part = pl.ds(row_at(b + u, 0), 8)
-                value = jnp.where(packed_left, arrived[0, part, :], arrived[1, part, :])
-                value = jnp.where(packed_inside, value, 0.0)
-                for f in range(F):
-                    field[H, f, pl.ds(row_at(b + u), 8), :] = rolled(value, -4 * (f - 2))
-
-        steps(0, blocks, run, 8)
+    def pack_block(field, b):
+        value = field[E, 2, pl.ds(row_at(b), 8), :]
+        for f in (0, 1, 3, 4):
+            at = 54 + 4 * f
+            mine = (lane >= at) & (lane < at + 4)
+            value = jnp.where(mine, rolled(field[E, f, pl.ds(row_at(b), 8), :], 4 * (f - 2)), value)
+        return value
+
+    def unpack_block(from_left, from_right, field, b):
+        value = jnp.where(packed_left, from_left, from_right)
+        value = jnp.where(packed_inside, value, 0.0)
+        for f in range(F):
+            field[H, f, pl.ds(row_at(b), 8), :] = rolled(value, -4 * (f - 2))
+
+    def pack_all(b, n):
+        for u in range(n):
+            packed[pl.ds(row_at(b + u, 0), 8), :] = pack_block(v0, b + u)
+
+    def unpack_all(b, n):
+        for u in range(n):
+            part = pl.ds(row_at(b + u, 0), 8)
+            unpack_block(halo[0, part, :], halo[1, part, :], v0, b + u)
+
+    def pair_blocks(k):
+        return [(c * per + u, slice(i * CH + u * 8, i * CH + u * 8 + 8))
+                for i, c in enumerate((k, chunks - 1 - k)) for u in range(per)]
+
+    def send_pair(k):
+        arrive(E, k)
+        arrive(E, chunks - 1 - k)
+        for b, part in pair_blocks(k):
+            packed2[k, part, :] = pack_block(w0, b)
+        for side in (0, 1):
+            pair_columns(k, side).start()
+
+    def take_pair(k):
+        for side in (0, 1):
+            pair_columns(k, side).wait()
+        for b, part in pair_blocks(k):
+            unpack_block(halo2[0, k, part, :], halo2[1, k, part, :], w0, b)
 
     @pl.loop(0, chunks)
     def _(c):
@@ -227,13 +253,8 @@
     for c in range(chunks):
         load(forcing, force, load_f, c).start()
     pl.semaphore_wait(barrier, 6)
-    for c in outer_first:
-        stream_a(E, c).start()
-    pack(v0, packed)
-    for side in (0, 1):
-        columns(0, side).start()
-    for c in outer_first:
-        stream_a(M, c).start()
+    for t, c in a_order:
+        stream_a(t, c).start()
     for copy in coefs:
         copy.wait()
     for c in range(chunks):
@@ -250,17 +271,24 @@
     keep = [1.0 - diff_ref[f] for f in range(F)]
     visc = [diff_ref[f] * 0.25 for f in range(F)]
 
-    first_step(v0, v1, fwd, (M, E), False, per - 1, 2)
-
-    @pl.loop(1, chunks - 1)
-    def _(c):
+    def no_halo(c):
         first_step(v0, v1, fwd, (M, E), False, c * per + 1, per)
         to_end((M,), True, c * per, per)
         stream_b(M, c).start()
 
-    for side in (0, 1):
-        columns(0, side).wait()
-    unpack(halo, v0)
+    first_step(v0, v1, fwd, (M, E), False, per - 1, 2)
+    no_halo(1)
+    steps(0, blocks, pack_all, 8)
+    for side in (0, 1):
+        columns(side).start()
+
+    @pl.loop(2, chunks - 1)
+    def _(c):
+        no_halo(c)
+
+    for side in (0, 1):
+        columns(side).wait()
+    steps(0, blocks, unpack_all, 8)
     for side in (0, 1):
         edge_rows(0, side).start()
     first_step(v0, v1, fwd, (E, H), True, per - 1, blocks - 2 * per + 2)
@@ -297,24 +325,6 @@
             part = pl.ds(row_at(b, 0), 8)
             for f in range(F):
                 w0[t, f, pl.ds(row_at(b), 8), :] = end[t, f, part, :] - got_a[t, f, part, :]
-
-    arrive(E, 0)
-    arrive(E, chunks - 1)
-
-    @pl.loop(1, chunks - 1)
-    def _(c):
-        arrive(E, c)
-
-    pack(w0, packed2)
-    for side in (0, 1):
-        columns(1, side).start()
-    arrive(M, 0)
-    arrive(M, chunks - 1)
-    for side in (0, 1):
-        columns(1, side).wait()
-    unpack(halo2, w0)
-    for side in (0, 1):
-        edge_rows(1, side).start()
 
     def out_rows(lo, count):
         def run(b, n):
@@ -339,8 +349,20 @@
 
         steps(lo, count, lambda b, n: stencil(w1, adj, b, n, (M, E), True, emit))
 
+    send_pair(0)
+    arrive(M, 0)
+    arrive(M, chunks - 1)
+    send_pair(1)
+    take_pair(0)
+    for side in (0, 1):
+        edge_rows(1, side).start()
+    send_pair(2)
+    take_pair(1)
     for side in (0, 1):
         edge_rows(1, side).wait()
+    send_pair(3)
+    take_pair(2)
+
     def arrive_b(c):
         stream_b(M, c).wait_recv()
         stream_b(E, c).wait_recv()
@@ -352,14 +374,17 @@
         arrive_b(i * (chunks - 1))
         adjoint_rows(i * (blocks - per + 2), per - 2)
 
-    @pl.loop(0, chunks - 3)
-    def _(j):
+    def inner_step(j):
         c, lower = inward(j)
         arrive(M, c)
         first_step(w0, w1, adj, (M, E, H), True, c * per - 1 + 2 * lower, per)
         out_rows(c * per, per)
         arrive_b(c)
         adjoint_rows(c * per - 2 + 4 * lower, per)
+
+    pl.loop(0, 2)(inner_step)
+    take_pair(3)
+    pl.loop(2, chunks - 3)(inner_step)
 
     arrive(M, half)
     first_step(w0, w1, adj, (M, E, H), True, half * per - 1, per + 2)
@@ -413,11 +438,11 @@
         scratch_shapes=[
             pltpu.SMEM((F, F), jnp.float32), pltpu.SMEM((F, F), jnp.float32), pltpu.SMEM((F,), jnp.float32),
             block, block, pltpu.VMEM((2, 3, F, CH, L), jnp.float32), tiles, tiles, tiles, tiles, pair, pair, pair,
-            pltpu.VMEM((rows, L), jnp.float32), pltpu.VMEM((rows, L), jnp.float32),
-            pltpu.VMEM((2, rows, L), jnp.float32), pltpu.VMEM((2, rows, L), jnp.float32),
+            pltpu.VMEM((rows, L), jnp.float32), pltpu.VMEM((chunks // 2, 2 * CH, L), jnp.float32),
+            pltpu.VMEM((2, rows, L), jnp.float32), pltpu.VMEM((2, chunks // 2, 2 * CH, L), jnp.float32),
             dma((3,)), dma((chunks,)), dma((chunks,)),
             dma((2, chunks)), dma((2, chunks)), dma((2, chunks)), dma((2, chunks)),
-            dma((2, 2)), dma((2, 2)), dma((2, 2)), dma((2, 2)),
+            dma((2,)), dma((2,)), dma((chunks // 2, 2)), dma((chunks // 2, 2)), dma((2, 2)), dma((2, 2)),
         ],
         compiler_params=pltpu.CompilerParams(collective_id=0, has_side_effects=True, vmem_limit_bytes=40 << 20),
         name="orbit",

time: 41.7 us -> 40.4 us (0.969)
  the two profiles are of different devices: /device:TPU:2 before, /device:TPU:97 now
where the time goes in v3:
time: 40.4 us; the launch traced here: 40.3 us
  Pallas kernels  37.5 us (93%)
  local copies, waits for them, and re-layouts  2.11 us (5%)
  between operations  0.64 us (2%)
    pallas_call x1, Pallas kernels, body(): pl.pallas_call(kernel, out_shape=(shape, shape), in_specs=[pl.BlockSpec(m...  37.5 us
    unnamed x2, local copies, waits for them, and re-layouts  2.11 us

profile of v3, /device:TPU:97, one launch (start us, length us, event | category | flops | bytes accessed | tf_op | source)
XLA Modules:
  0.0 40.3 jit_solution(13117399476470442371)
XLA Ops:
  0.6 37.5 %orbit.1 = (f32[1,5,256,256]{3,2,1,0:T(8,128)S(1)}, f32[1,5,256,256]{3,2,1,0:T(8,128)S(1)}) custom-call(f32[1,5,256,256]{3,2,1,0:T(8,128)} %states.1, f32[1,5,256,256]{3,2,1,0:T(8,128)} %forcing.1, f32[5,5]{1,0:T(8,128)} %pitch_hbm.1, f32[5,5]{1,0:T(8,128)} %span_hbm.1, f32[5]{0:T(128)} %diff_hbm.1), custom_call_target="tpu_custom_call" | custom-call | tf_op jit(solution)/shard_map/orbit/pallas_call | solution.py:433
  38.1 1.1 %copy.9 = f32[1,5,256,256]{3,2,1,0:T(8,128)} copy(f32[1,5,256,256]{3,2,1,0:T(8,128)S(1)} %get-tuple-element.4) | data formatting | bytes 2621440
  39.2 1.1 %copy.10 = f32[1,5,256,256]{3,2,1,0:T(8,128)} copy(f32[1,5,256,256]{3,2,1,0:T(8,128)S(1)} %get-tuple-element.5) | data formatting | bytes 2621440

commit v4 on v3

--- a/solution.py
+++ b/solution.py
@@ -418,6 +418,18 @@
             stream_b(t, c).wait_send()
 
 
+def store(mis, grad, mis_out, grad_out, sem):
+    copies = [
+        pltpu.make_async_copy(src.at[0, f], dst.at[0, f], sem.at[i, f])
+        for f in range(F)
+        for i, (src, dst) in enumerate(((mis, mis_out), (grad, grad_out)))
+    ]
+    for copy in copies:
+        copy.start()
+    for copy in copies:
+        copy.wait()
+
+
 def body(states, forcing, adv_pitch, adv_span, diffusion):
     states, forcing, adv_pitch, adv_span, diffusion = (
         pltpu.with_memory_space_constraint(x, pltpu.HBM) for x in (states, forcing, adv_pitch, adv_span, diffusion)
@@ -430,7 +442,7 @@
     tiles = pltpu.VMEM((3, F, tall, L), jnp.float32)
     pair = pltpu.VMEM((2, F, rows, L), jnp.float32)
     block = pltpu.VMEM((F, rows, 2 * L), jnp.float32)
-    return pl.pallas_call(
+    results = pl.pallas_call(
         kernel,
         out_shape=(shape, shape),
         in_specs=[pl.BlockSpec(memory_space=pltpu.HBM)] * 5,
@@ -447,6 +459,15 @@
         compiler_params=pltpu.CompilerParams(collective_id=0, has_side_effects=True, vmem_limit_bytes=40 << 20),
         name="orbit",
     )(states, forcing, adv_pitch, adv_span, diffusion)
+    return pl.pallas_call(
+        store,
+        out_shape=(shape, shape),
+        in_specs=[pl.BlockSpec(memory_space=pltpu.VMEM)] * 2,
+        out_specs=[pl.BlockSpec(memory_space=pltpu.HBM)] * 2,
+        scratch_shapes=[dma((2, F))],
+        compiler_params=pltpu.CompilerParams(vmem_limit_bytes=4 << 20),
+        name="store",
+    )(*results)
 
 
 def solution(mesh):

time: 40.4 us -> 39.8 us (0.985)
  local copies, waits for them, and re-layouts: 2.11 us -> 0 us
  Pallas kernels: 37.5 us -> 39.1 us
    unnamed x2 -> x0, local copies, waits for them, and re-layouts: 2.11 us -> none
    pallas_call x0 -> x1, Pallas kernels: none -> 1.57 us  [body(): pl.pallas_call(store, out_shape=(shape, shape), in_specs=[pl.BlockSpec(me...]
where the time goes in v4:
time: 39.8 us; the launch traced here: 39.7 us
  Pallas kernels  39.1 us (98%)
  between operations  0.64 us (2%)
    pallas_call x1, Pallas kernels, body(): pl.pallas_call(kernel, out_shape=(shape, shape), in_specs=[pl.BlockSpec(m...  37.5 us
    pallas_call x1, Pallas kernels, body(): pl.pallas_call(store, out_shape=(shape, shape), in_specs=[pl.BlockSpec(me...  1.57 us

profile of v4, /device:TPU:97, one launch (start us, length us, event | category | flops | bytes accessed | tf_op | source)
XLA Modules:
  0.0 39.7 jit_solution(3957278047339669502)
XLA Ops:
  0.6 37.5 %orbit.1 = (f32[1,5,256,256]{3,2,1,0:T(8,128)S(1)}, f32[1,5,256,256]{3,2,1,0:T(8,128)S(1)}) custom-call(f32[1,5,256,256]{3,2,1,0:T(8,128)} %states.1, f32[1,5,256,256]{3,2,1,0:T(8,128)} %forcing.1, f32[5,5]{1,0:T(8,128)} %pitch_hbm.1, f32[5,5]{1,0:T(8,128)} %span_hbm.1, f32[5]{0:T(128)} %diff_hbm.1), custom_call_target="tpu_custom_call" | custom-call | tf_op jit(solution)/shard_map/orbit/pallas_call | solution.py:445
  38.1 1.6 %store.1 = (f32[1,5,256,256]{3,2,1,0:T(8,128)}, f32[1,5,256,256]{3,2,1,0:T(8,128)}) custom-call(f32[1,5,256,256]{3,2,1,0:T(8,128)S(1)} %get-tuple-element.4.mis, f32[1,5,256,256]{3,2,1,0:T(8,128)S(1)} %get-tuple-element.5.grad), custom_call_target="tpu_custom_call" | custom-call | tf_op jit(solution)/shard_map/store/pallas_call | solution.py:462

commit v5 on v4

--- a/solution.py
+++ b/solution.py
@@ -28,6 +28,7 @@
     states, forcing, pitch_hbm, span_hbm, diff_hbm, mis_out, grad_out,
     pitch_ref, span_ref, diff_ref, raw, force, across, v0, v1, w0, w1, end, got_a, got_b, packed, packed2, halo, halo2,
     load_c, load_s, load_f, a_send, a_recv, b_send, b_recv, col_send, col_recv, pair_send, pair_recv, row_send, row_recv,
+    half_send, half_recv,
 ):
     rows = raw.shape[1]
     chunks = rows // CH
@@ -36,7 +37,7 @@
     per = CH // 8
     half = chunks // 2
     outer_first = [c for i in range(half) for c in (i, chunks - 1 - i)]
-    a_order = [(t, c) for part in (outer_first[:2], outer_first[2:]) for t in (E, M) for c in part]
+    a_order = [(t, c) for part in (outer_first[:2], outer_first[2:]) for t in (E, M) for c in part if (t, c) != (M, half)]
 
     def load(src, dst, sem, c):
         part = pl.ds(c * CH, CH)
@@ -44,6 +45,7 @@
 
     for c in range(chunks):
         load(states, raw, load_s, c).start()
+    load(forcing, force, load_f, 1).start()
     coefs = [
         pltpu.make_async_copy(src, dst, load_c.at[i])
         for i, (src, dst) in enumerate(((pitch_hbm, pitch_ref), (span_hbm, span_ref), (diff_hbm, diff_ref)))
@@ -164,6 +166,14 @@
             device_id=along("seg", -1), device_id_type=MESH,
         )
 
+    def half_chunk(i):
+        first = half * CH + i * CH // 2
+        return pltpu.make_async_remote_copy(
+            src_ref=v0.at[M, :, pl.ds(PAD + first, CH // 2)], dst_ref=got_a.at[M, :, pl.ds(first, CH // 2)],
+            send_sem=half_send.at[i], recv_sem=half_recv.at[i],
+            device_id=along("seg", -1), device_id_type=MESH,
+        )
+
     def stream_b(t, c):
         part = pl.ds(pl.multiple_of(c * CH, 8), CH)
         return pltpu.make_async_remote_copy(
@@ -250,15 +260,10 @@
                 v0[M, f, pl.ds(row_at(b), 8), :] = mid
                 v0[E, f, pl.ds(row_at(b), 8), :] = edge
 
-    for c in range(chunks):
+    for c in [0] + list(range(2, chunks)):
         load(forcing, force, load_f, c).start()
-    pl.semaphore_wait(barrier, 6)
-    for t, c in a_order:
-        stream_a(t, c).start()
     for copy in coefs:
         copy.wait()
-    for c in range(chunks):
-        load(forcing, force, load_f, c).wait()
 
     fwd = (
         [[pitch_ref[f, g] * -0.125 for g in range(F)] for f in range(F)],
@@ -274,10 +279,18 @@
     def no_halo(c):
         first_step(v0, v1, fwd, (M, E), False, c * per + 1, per)
         to_end((M,), True, c * per, per)
-        stream_b(M, c).start()
 
     first_step(v0, v1, fwd, (M, E), False, per - 1, 2)
+    load(forcing, force, load_f, 1).wait()
     no_halo(1)
+    pl.semaphore_wait(barrier, 6)
+    stream_b(M, 1).start()
+    for t, c in a_order:
+        stream_a(t, c).start()
+    for i in (1, 0):
+        half_chunk(i).start()
+    for c in [0] + list(range(2, chunks)):
+        load(forcing, force, load_f, c).wait()
     steps(0, blocks, pack_all, 8)
     for side in (0, 1):
         columns(side).start()
@@ -285,6 +298,7 @@
     @pl.loop(2, chunks - 1)
     def _(c):
         no_halo(c)
+        stream_b(M, c).start()
 
     for side in (0, 1):
         columns(side).wait()
@@ -317,14 +331,15 @@
         to_end((E,), False, c * per, per)
         stream_b(E, c).start()
 
+    def take_mismatch(t, b, n):
+        for u in range(n):
+            part = pl.ds(row_at(b + u, 0), 8)
+            for f in range(F):
+                w0[t, f, pl.ds(row_at(b + u), 8), :] = end[t, f, part, :] - got_a[t, f, part, :]
+
     def arrive(t, c):
         stream_a(t, c).wait_recv()
-
-        for u in range(per):
-            b = c * per + u
-            part = pl.ds(row_at(b, 0), 8)
-            for f in range(F):
-                w0[t, f, pl.ds(row_at(b), 8), :] = end[t, f, part, :] - got_a[t, f, part, :]
+        take_mismatch(t, c * per, per)
 
     def out_rows(lo, count):
         def run(b, n):
@@ -386,16 +401,26 @@
     take_pair(3)
     pl.loop(2, chunks - 3)(inner_step)
 
-    arrive(M, half)
-    first_step(w0, w1, adj, (M, E, H), True, half * per - 1, per + 2)
-    out_rows(half * per, per)
+    at = half * per
+    first_step(w0, w1, adj, (H,), True, at - 1, per + 2)
+    for c in range(chunks):
+        stream_a(E, c).wait_send()
+        stream_b(M, c).wait_send()
+    half_chunk(1).wait_recv()
+    take_mismatch(M, at + per // 2, per // 2)
+    first_step(w0, w1, adj, (M, E), True, at + per - 1, 2)
+    adjoint_rows(at + per, 2)
+    half_chunk(0).wait_recv()
+    take_mismatch(M, at, per // 2)
+    first_step(w0, w1, adj, (M, E), True, at - 1, per)
+    out_rows(at, per)
 
     def keep_adjoint(b, total):
         for f in range(F):
             for t in (M, E):
                 w0[t, f, pl.ds(row_at(b), 8), :] = total[t][f]
 
-    steps(half * per - 2, per + 4, lambda b, n: stencil(w1, adj, b, n, (M, E), True, keep_adjoint))
+    steps(at - 2, per + 2, lambda b, n: stencil(w1, adj, b, n, (M, E), True, keep_adjoint))
     arrive_b(half)
 
     def last_rows(b, n):
@@ -409,13 +434,18 @@
                 grad_out[0, f, part, 0:L] = one
                 grad_out[0, f, part, L : 2 * L] = two
 
-    steps(half * per - 2, per + 4, last_rows)
-
-    for t in (M, E):
-        @pl.loop(0, chunks)
-        def _(c):
-            stream_a(t, c).wait_send()
-            stream_b(t, c).wait_send()
+    steps(at - 2, per + 2, last_rows)
+
+    for i in (0, 1):
+        half_chunk(i).wait_send()
+
+    @pl.loop(0, chunks - 1)
+    def _(i):
+        stream_a(M, jnp.where(i < half, i, i + 1)).wait_send()
+
+    @pl.loop(0, chunks)
+    def _(c):
+        stream_b(E, c).wait_send()
 
 
 def store(mis, grad, mis_out, grad_out, sem):
@@ -455,6 +485,7 @@
             dma((3,)), dma((chunks,)), dma((chunks,)),
             dma((2, chunks)), dma((2, chunks)), dma((2, chunks)), dma((2, chunks)),
             dma((2,)), dma((2,)), dma((chunks // 2, 2)), dma((chunks // 2, 2)), dma((2, 2)), dma((2, 2)),
+            dma((2,)), dma((2,)),
         ],
         compiler_params=pltpu.CompilerParams(collective_id=0, has_side_effects=True, vmem_limit_bytes=40 << 20),
         name="orbit",

time: 39.8 us -> 39.4 us (0.990)
  Pallas kernels: 39.1 us -> 38.6 us
    pallas_call x1, Pallas kernels: 37.5 us -> 37 us  [body(): pl.pallas_call(kernel, out_shape=(shape, shape), in_specs=[pl.BlockSpec(m...]
where the time goes in v5:
time: 39.4 us; the launch traced here: 39.3 us
  Pallas kernels  38.6 us (98%)
  between operations  0.64 us (2%)
    pallas_call x1, Pallas kernels, body(): pl.pallas_call(kernel, out_shape=(shape, shape), in_specs=[pl.BlockSpec(m...  37 us
    pallas_call x1, Pallas kernels, body(): pl.pallas_call(store, out_shape=(shape, shape), in_specs=[pl.BlockSpec(me...  1.57 us

profile of v5, /device:TPU:97, one launch (start us, length us, event | category | flops | bytes accessed | tf_op | source)
XLA Modules:
  0.0 39.3 jit_solution(12222048226256620058)
XLA Ops:
  0.6 37.0 %orbit.1 = (f32[1,5,256,256]{3,2,1,0:T(8,128)S(1)}, f32[1,5,256,256]{3,2,1,0:T(8,128)S(1)}) custom-call(f32[1,5,256,256]{3,2,1,0:T(8,128)} %states.1, f32[1,5,256,256]{3,2,1,0:T(8,128)} %forcing.1, f32[5,5]{1,0:T(8,128)} %pitch_hbm.1, f32[5,5]{1,0:T(8,128)} %span_hbm.1, f32[5]{0:T(128)} %diff_hbm.1), custom_call_target="tpu_custom_call" | custom-call | tf_op jit(solution)/shard_map/orbit/pallas_call | solution.py:475
  37.7 1.6 %store.1 = (f32[1,5,256,256]{3,2,1,0:T(8,128)}, f32[1,5,256,256]{3,2,1,0:T(8,128)}) custom-call(f32[1,5,256,256]{3,2,1,0:T(8,128)S(1)} %get-tuple-element.4.mis, f32[1,5,256,256]{3,2,1,0:T(8,128)S(1)} %get-tuple-element.5.grad), custom_call_target="tpu_custom_call" | custom-call | tf_op jit(solution)/shard_map/store/pallas_call | solution.py:493

commit v6 on v5

--- a/solution.py
+++ b/solution.py
@@ -43,6 +43,11 @@
         part = pl.ds(c * CH, CH)
         return pltpu.make_async_copy(src.at[0, :, part], dst.at[:, part], sem.at[c])
 
+    barrier = pltpu.get_barrier_semaphore()
+    for axis in ("seg", "pitch", "span"):
+        for by in (1, -1):
+            pl.semaphore_signal(barrier, inc=1, device_id=along(axis, by), device_id_type=MESH)
+
     for c in range(chunks):
         load(states, raw, load_s, c).start()
     load(forcing, force, load_f, 1).start()
@@ -52,11 +57,6 @@
     ]
     for copy in coefs:
         copy.start()
-
-    barrier = pltpu.get_barrier_semaphore()
-    for axis in ("seg", "pitch", "span"):
-        for by in (1, -1):
-            pl.semaphore_signal(barrier, inc=1, device_id=along(axis, by), device_id_type=MESH)
 
     lane = lax.broadcasted_iota(jnp.int32, (8, L), 1)
     low = lane < 64

time: 39.4 us -> 39.3 us (level)
  no operation moved by 1% of the time
where the time goes in v6:
time: 39.3 us; the launch traced here: 39.2 us
  Pallas kernels  38.5 us (98%)
  between operations  0.64 us (2%)
    pallas_call x1, Pallas kernels, body(): pl.pallas_call(kernel, out_shape=(shape, shape), in_specs=[pl.BlockSpec(m...  37 us
    pallas_call x1, Pallas kernels, body(): pl.pallas_call(store, out_shape=(shape, shape), in_specs=[pl.BlockSpec(me...  1.57 us

profile of v6, /device:TPU:97, one launch (start us, length us, event | category | flops | bytes accessed | tf_op | source)
XLA Modules:
  0.0 39.2 jit_solution(9493930552595510996)
XLA Ops:
  0.6 37.0 %orbit.1 = (f32[1,5,256,256]{3,2,1,0:T(8,128)S(1)}, f32[1,5,256,256]{3,2,1,0:T(8,128)S(1)}) custom-call(f32[1,5,256,256]{3,2,1,0:T(8,128)} %states.1, f32[1,5,256,256]{3,2,1,0:T(8,128)} %forcing.1, f32[5,5]{1,0:T(8,128)} %pitch_hbm.1, f32[5,5]{1,0:T(8,128)} %span_hbm.1, f32[5]{0:T(128)} %diff_hbm.1), custom_call_target="tpu_custom_call" | custom-call | tf_op jit(solution)/shard_map/orbit/pallas_call | solution.py:475
  37.6 1.6 %store.1 = (f32[1,5,256,256]{3,2,1,0:T(8,128)}, f32[1,5,256,256]{3,2,1,0:T(8,128)}) custom-call(f32[1,5,256,256]{3,2,1,0:T(8,128)S(1)} %get-tuple-element.4.mis, f32[1,5,256,256]{3,2,1,0:T(8,128)S(1)} %get-tuple-element.5.grad), custom_call_target="tpu_custom_call" | custom-call | tf_op jit(solution)/shard_map/store/pallas_call | solution.py:493
